TPU v7x, 32 devices: a whole 2x2x4 slice. The times are simulated.
32 devices in a mesh: dp: 2 (over x), ctx: 16 (over z, y, core).
Axes of the slice: x: 2, y: 2, z: 4, core: 2. Of those that a mesh axis runs over, the one named last changes fastest.
Arguments:
- features: bfloat16 [2, 2048, 1536], P('dp', 'ctx'), may hold values from -500 to 500
- gain: float32 [1536], replicated, may hold values from 0.1 to 1.9
- conv_weight: bfloat16 [5, 1536, 768], replicated, may hold values from -0.0625 to 0.0625
- cotangent: bfloat16 [2, 2048, 768], P('dp', 'ctx'), may hold values from -15 to 15
Outputs:
- convolved: bfloat16 [2, 2048, 768], P('dp', 'ctx')
- input_grad: bfloat16 [2, 2048, 1536], P('dp', 'ctx')
- gain_grad: float32 [1536], replicated
All inputs are finite; a program needn't handle non-finite values.
Results may differ from a plain program's by a relative error of at most 0.0054.
Values may be sent and summed in bfloat16 or wider, within the bound.
A program may use at most 64 MiB of HBM per device.

v0:
```python
import math

import jax
import jax.numpy as jnp
from jax import lax
from jax.sharding import PartitionSpec as P

KERNEL_TAPS = 5


EPS = 1e-06


def shifted(block, axis, distance):
    devices = range(lax.axis_size(axis))
    route = [(i - distance, i) for i in devices if i - distance in devices]
    return lax.ppermute(block, axis, route)


def activate(values):
    return jax.nn.gelu(values, approximate=True)


def flip_channels(values):
    return values[:, :, ::-1]


def taps_ahead(values, shard_hops):
    pieces = []
    for tap_index in range(KERNEL_TAPS):
        if tap_index == KERNEL_TAPS // 2:
            pieces.append(values)
        else:
            pieces.append(shifted(values, "ctx", -(tap_index - KERNEL_TAPS // 2) * shard_hops))
    return pieces


def taps_behind(values, shard_hops):
    pieces = []
    for tap_index in range(KERNEL_TAPS):
        if tap_index == KERNEL_TAPS // 2:
            pieces.append(values)
        else:
            pieces.append(shifted(values, "ctx", (tap_index - KERNEL_TAPS // 2) * shard_hops))
    return pieces


def apply_forward(pieces, weight):
    lead = pieces[0].shape[0]
    middle = pieces[0].shape[1]
    total = jnp.zeros((lead * middle, weight.shape[2]), jnp.float32)
    for tap_index in range(KERNEL_TAPS):
        flat_rows = pieces[tap_index].reshape(lead * middle, pieces[tap_index].shape[2])
        total = total + jnp.dot(flat_rows, weight[tap_index], preferred_element_type=jnp.float32)
    return total.reshape(lead, middle, weight.shape[2])


def apply_backward(pieces, weight):
    lead = pieces[0].shape[0]
    middle = pieces[0].shape[1]
    total = jnp.zeros((lead * middle, weight.shape[1]), jnp.float32)
    for tap_index in range(KERNEL_TAPS):
        flat_rows = pieces[tap_index].reshape(lead * middle, pieces[tap_index].shape[2])
        total = total + lax.dot_general(
            flat_rows,
            weight[tap_index],
            (((1,), (1,)), ((), ())),
            preferred_element_type=jnp.float32,
        )
    return total.reshape(lead, middle, weight.shape[1])


def per_device(features, gain, conv_weight, cotangent):
    shard_hops = lax.axis_size("ctx") // 8
    wide = features.astype(jnp.float32)
    inv_rms = lax.rsqrt(jnp.mean(wide * wide, axis=-1, keepdims=True) + EPS)
    normed = wide * inv_rms
    scaled = normed * gain
    hidden = activate(scaled).astype(jnp.bfloat16)
    ahead = taps_ahead(hidden, shard_hops)
    forward_term = apply_forward(ahead, conv_weight)
    flipped = [
        flip_channels(ahead[KERNEL_TAPS - 1 - tap_index]) for tap_index in range(KERNEL_TAPS)
    ]
    reverse_term = flip_channels(apply_forward(flipped, conv_weight).astype(jnp.bfloat16))
    convolved = (forward_term + reverse_term.astype(jnp.float32)).astype(jnp.bfloat16)
    behind = taps_behind(cotangent, shard_hops)
    back_forward = apply_backward(behind, conv_weight)
    flipped_grads = [
        flip_channels(behind[KERNEL_TAPS - 1 - tap_index]) for tap_index in range(KERNEL_TAPS)
    ]
    back_reverse = flip_channels(apply_backward(flipped_grads, conv_weight).astype(jnp.bfloat16))
    grad_hidden = back_forward + back_reverse.astype(jnp.float32)
    _, pullback = jax.vjp(activate, scaled)
    grad_scaled = pullback(grad_hidden)[0]
    partial_sum = jnp.sum(grad_scaled * normed, axis=(0, 1))
    summed = lax.psum(partial_sum, ("dp", "ctx"))
    total_rows = features.shape[0] * features.shape[1] * lax.axis_size("dp") * lax.axis_size("ctx")
    gain_grad = summed / math.sqrt(total_rows)
    grad_normed = grad_scaled * gain
    spread_term = jnp.mean(grad_normed * normed, axis=-1, keepdims=True)
    input_grad = (inv_rms * (grad_normed - normed * spread_term)).astype(jnp.bfloat16)
    return (convolved, input_grad, gain_grad)


def solution(mesh):
    return jax.shard_map(
        per_device,
        mesh=mesh,
        in_specs=(P("dp", "ctx", None), P(), P(), P("dp", "ctx", None)),
        out_specs=(P("dp", "ctx", None), P("dp", "ctx", None), P()),
        check_vma=False,
    )
```

profile of v0, /device:TPU:0, one launch (start us, length us, event | category | flops | bytes accessed | tf_op | source)
XLA Modules:
  0.0 152.5 jit_solution(12865565920787407074)
XLA Ops:
  0.6 4.9 %collective-permute-start.6 = (bf16[1,128,768]{2,1,0:T(8,128)(2,1)}, bf16[1,128,768]{2,1,0:T(8,128)(2,1)S(1)}, u32[]{:S(2)}, u32[]{:S(2)}) collective-permute-start(bf16[1,128,768]{2,1,0:T(8,128)(2,1)} %param.7), channel_id=1, source_target_pairs={{0,2},{1,3},{2,4},{3,5},{4,6},{5,7},{6,8},{7,9},{8,10},{9,11},{10,... | collective-permute-start | bytes 589832 | tf_op jit(solution)/shard_map/ppermute | solution.py:17
  5.5 3.5 %collective-permute-start.7 = (bf16[1,128,768]{2,1,0:T(8,128)(2,1)}, bf16[1,128,768]{2,1,0:T(8,128)(2,1)S(1)}, u32[]{:S(2)}, u32[]{:S(2)}) collective-permute-start(bf16[1,128,768]{2,1,0:T(8,128)(2,1)} %param.7), channel_id=1, source_target_pairs={{0,4},{1,5},{2,6},{3,7},{4,8},{5,9},{6,10},{7,11},{8,12},{9,13},{1... | collective-permute-start | bytes 589832 | tf_op jit(solution)/shard_map/ppermute | solution.py:17
  9.0 1.3 collective-permute-start.4
  10.3 1.3 collective-permute-start.5
  11.6 2.7 %rev.39 = bf16[1,128,768]{2,1,0:T(8,128)(2,1)S(1)} reverse(bf16[1,128,768]{2,1,0:T(8,128)(2,1)} %param.7), dimensions={2} | reverse | bytes 393216 | tf_op jit(solution)/shard_map/rev | solution.py:25
  14.3 2.7 %fusion.23 = f32[128,1536]{1,0:T(8,128)S(1)} fusion(bf16[5,1536,768]{2,1,0:T(8,128)(2,1)} %param.6, bf16[1,128,768]{2,1,0:T(8,128)(2,1)} %param.7), kind=kOutput, calls=%fused_computation.27 | convolution fusion | flops 301989888 | bytes 3342336 | tf_op jit(solution)/shard_map/dot_general | solution.py:64
  17.0 2.6 %fusion.21 = f32[128,1536]{1,0:T(8,128)S(1)} fusion(bf16[5,1536,768]{2,1,0:T(8,128)(2,1)} %param.6, bf16[1,128,768]{2,1,0:T(8,128)(2,1)S(1)} %rev.39), kind=kOutput, calls=%fused_computation.25 | convolution fusion | flops 301989888 | bytes 3342336 | tf_op jit(solution)/shard_map/dot_general | solution.py:64
  19.5 1.2 fusion.116
  20.7 0.6 rev.38
  21.4 2.5 %fusion.29 = f32[128,1536]{1,0:T(8,128)S(1)} fusion(bf16[5,1536,768]{2,1,0:T(8,128)(2,1)} %param.6, bf16[1,128,768]{2,1,0:T(8,128)(2,1)S(1)} %rev.38), kind=kOutput, calls=%fused_computation.33 | convolution fusion | flops 301989888 | bytes 3342336 | tf_op jit(solution)/shard_map/dot_general | solution.py:64
  23.9 0.0 copy-start.1
  24.0 0.7 copy-done.1
  24.6 2.2 %rev.37 = bf16[1,128,768]{2,1,0:T(8,128)(2,1)} reverse(bf16[1,128,768]{2,1,0:T(8,128)(2,1)S(1)} %collective-permute-done.7), dimensions={2} | reverse | bytes 393216 | tf_op jit(solution)/shard_map/rev | solution.py:25
  26.8 2.7 %fusion.1 = f32[128,1536]{1,0:T(8,128)S(1)} fusion(f32[128,1536]{1,0:T(8,128)S(1)} %fusion.21, f32[128,1536]{1,0:T(8,128)S(1)} %fusion.29, bf16[5,1536,768]{2,1,0:T(8,128)(2,1)} %param.6, bf16[1,128,768]{2,1,0:T(8,128)(2,1)} %rev.37), kind=kOutput, calls=%fused_computation.3 | convolution fusion | flops 302383104 | bytes 4915200 | tf_op jit(solution)/shard_map/dot_general | solution.py:64
  29.6 0.0 copy-start.2
  29.6 2.7 %rev.41 = bf16[1,128,768]{2,1,0:T(8,128)(2,1)S(1)} reverse(bf16[1,128,768]{2,1,0:T(8,128)(2,1)} %collective-permute-done.4), dimensions={2} | reverse | bytes 393216 | tf_op jit(solution)/shard_map/rev | solution.py:25
  32.3 2.6 %fusion.7 = f32[128,1536]{1,0:T(8,128)S(1)} fusion(bf16[5,1536,768]{2,1,0:T(8,128)(2,1)} %param.6, bf16[1,128,768]{2,1,0:T(8,128)(2,1)S(1)} %rev.41), kind=kOutput, calls=%fused_computation.11 | convolution fusion | flops 301989888 | bytes 3342336 | tf_op jit(solution)/shard_map/dot_general | solution.py:64
  34.8 0.0 collective-permute-done.5
  34.9 2.7 %rev.40 = bf16[1,128,768]{2,1,0:T(8,128)(2,1)S(1)} reverse(bf16[1,128,768]{2,1,0:T(8,128)(2,1)} %collective-permute-done.5), dimensions={2} | reverse | bytes 393216 | tf_op jit(solution)/shard_map/rev | solution.py:25
  37.5 2.6 %fusion.6 = bf16[128,1536]{1,0:T(8,128)(2,1)S(1)} fusion(f32[128,1536]{1,0:T(8,128)S(1)} %fusion.7, f32[128,1536]{1,0:T(8,128)S(1)} %fusion.1, bf16[5,1536,768]{2,1,0:T(8,128)(2,1)} %param.6, bf16[1,128,768]{2,1,0:T(8,128)(2,1)S(1)} %rev.40), kind=kOutput, calls=%fused_computation.10 | convolution fusion | flops 302579712 | bytes 4521984 | tf_op jit(solution)/shard_map/dot_general | solution.py:64
  40.1 1.2 reverse.7
  41.3 2.7 %fusion.31 = f32[128,1536]{1,0:T(8,128)S(1)} fusion(bf16[5,1536,768]{2,1,0:T(8,128)(2,1)} %param.6, bf16[1,128,768]{2,1,0:T(8,128)(2,1)} %collective-permute-done.5), kind=kOutput, calls=%fused_computation.35 | convolution fusion | flops 301989888 | bytes 3342336 | tf_op jit(solution)/shard_map/dot_general | solution.py:64
  44.0 2.5 %fusion.9 = f32[128,1536]{1,0:T(8,128)S(1)} fusion(bf16[5,1536,768]{2,1,0:T(8,128)(2,1)} %param.6, bf16[1,128,768]{2,1,0:T(8,128)(2,1)S(1)} %copy-done.2), kind=kOutput, calls=%fused_computation.13 | convolution fusion | flops 301989888 | bytes 3342336 | tf_op jit(solution)/shard_map/dot_general | solution.py:64
  46.5 2.7 %fusion.4 = f32[128,1536]{1,0:T(8,128)S(1)} fusion(f32[128,1536]{1,0:T(8,128)S(1)} %fusion.23, f32[128,1536]{1,0:T(8,128)S(1)} %fusion.31, bf16[5,1536,768]{2,1,0:T(8,128)(2,1)} %param.6, bf16[1,128,768]{2,1,0:T(8,128)(2,1)} %collective-permute-done.4), kind=kOutput, calls=%fused_computation.8 | convolution fusion | flops 302383104 | bytes 4915200 | tf_op jit(solution)/shard_map/dot_general | solution.py:64
  49.3 3.1 %fusion.115 = (f32[1536]{0:T(1024)S(1)}, f32[128]{0:T(128)S(1)}, f32[1,128,1536]{2,1,0:T(8,128)S(1)}) fusion(bf16[1,128,1536]{2,1,0:T(8,128)(2,1)S(1)} %copy-done, f32[128]{0:T(128)S(1)} %add_rsqrt_fusion, f32[1536]{0:T(1024)S(1)} %copy-done.5, bf16[128,1536]{1,0:T(8,128)(2,1)S(1)} %reverse.7, f32[128,1536]{1,0:T(8,128)S(1)} %fusion.9, ...), kind=kOutput, calls=%fused_computation.99 | convolution fusion | flops 308083072 | bytes 5714944 | tf_op jit(solution)/shard_map/dot_general | solution.py:64
  52.4 1.3 fusion.114
  53.7 5.5 %collective-permute-start = (bf16[1,128,1536]{2,1,0:T(8,128)(2,1)S(1)}, bf16[1,128,1536]{2,1,0:T(8,128)(2,1)S(1)}, u32[]{:S(2)}, u32[]{:S(2)}) collective-permute-start(bf16[1,128,1536]{2,1,0:T(8,128)(2,1)S(1)} %get-tuple-element.6), channel_id=1, source_target_pairs={{0,4},{1,5},{2,6},{3,7},{4,8},{5,9},{6,10},{7,11},{8,12},{9,13},{1... | collective-permute-start | bytes 1179656 | tf_op jit(solution)/shard_map/ppermute | solution.py:17
  59.2 3.6 %collective-permute-start.1 = (bf16[1,128,1536]{2,1,0:T(8,128)(2,1)S(1)}, bf16[1,128,1536]{2,1,0:T(8,128)(2,1)S(1)}, u32[]{:S(2)}, u32[]{:S(2)}) collective-permute-start(bf16[1,128,1536]{2,1,0:T(8,128)(2,1)S(1)} %get-tuple-element.6), channel_id=1, source_target_pairs={{0,2},{1,3},{2,4},{3,5},{4,6},{5,7},{6,8},{7,9},{8,10},{9,11},{10,... | collective-permute-start | bytes 1179656 | tf_op jit(solution)/shard_map/ppermute | solution.py:17
  62.8 1.3 collective-permute-start.2
  64.1 1.3 collective-permute-start.3
  65.4 1.2 rev.34
  66.6 2.1 %fusion.27 = f32[128,768]{1,0:T(8,128)S(1)} fusion(bf16[5,1536,768]{2,1,0:T(8,128)(2,1)} %param.6, bf16[1,128,1536]{2,1,0:T(8,128)(2,1)S(1)} %get-tuple-element.6), kind=kOutput, calls=%fused_computation.31 | convolution fusion | flops 301989888 | bytes 3145728 | tf_op jit(solution)/shard_map/dot_general | solution.py:54
  68.8 47.5 %psum.7 = f32[1536]{0:T(1024)S(1)} all-reduce(f32[1536]{0:T(1024)S(1)} %get-tuple-element.3), channel_id=1, replica_groups=mesh['dp'=2,'ctx'=16] {'dp','ctx'}, use_global_device_ids=true, to_apply=%region_3.0 | all-reduce | flops 1536 | bytes 12288 | tf_op jit(solution)/shard_map/psum | solution.py:97
  116.3 2.1 %fusion.25 = f32[128,768]{1,0:T(8,128)S(1)} fusion(bf16[5,1536,768]{2,1,0:T(8,128)(2,1)} %param.6, bf16[1,128,1536]{2,1,0:T(8,128)(2,1)S(1)} %rev.34), kind=kOutput, calls=%fused_computation.29 | convolution fusion | flops 301989888 | bytes 3145728 | tf_op jit(solution)/shard_map/dot_general | solution.py:54
  118.5 0.6 broadcast_multiply_fusion
  119.1 1.2 rev.36
  120.3 2.1 %fusion.11 = f32[128,768]{1,0:T(8,128)S(1)} fusion(bf16[5,1536,768]{2,1,0:T(8,128)(2,1)} %param.6, bf16[1,128,1536]{2,1,0:T(8,128)(2,1)S(1)} %rev.36), kind=kOutput, calls=%fused_computation.15 | convolution fusion | flops 301989888 | bytes 3145728 | tf_op jit(solution)/shard_map/dot_general | solution.py:54
  122.5 1.2 rev.35
  123.7 2.1 %fusion.17 = f32[128,768]{1,0:T(8,128)S(1)} fusion(bf16[5,1536,768]{2,1,0:T(8,128)(2,1)} %param.6, bf16[1,128,1536]{2,1,0:T(8,128)(2,1)S(1)} %rev.35), kind=kOutput, calls=%fused_computation.21 | convolution fusion | flops 301989888 | bytes 3145728 | tf_op jit(solution)/shard_map/dot_general | solution.py:54
  125.9 6.7 %rev.33 = bf16[1,128,1536]{2,1,0:T(8,128)(2,1)} reverse(bf16[1,128,1536]{2,1,0:T(8,128)(2,1)} %collective-permute-done.2), dimensions={2} | reverse | bytes 786432 | tf_op jit(solution)/shard_map/rev | solution.py:25
  132.6 2.3 %fusion.33 = f32[128,768]{1,0:T(8,128)S(1)} fusion(bf16[5,1536,768]{2,1,0:T(8,128)(2,1)} %param.6, bf16[1,128,1536]{2,1,0:T(8,128)(2,1)} %rev.33), kind=kOutput, calls=%fused_computation.37 | convolution fusion | flops 301989888 | bytes 3145728 | tf_op jit(solution)/shard_map/dot_general | solution.py:54
  134.9 5.2 %rev.32 = bf16[1,128,1536]{2,1,0:T(8,128)(2,1)S(1)} reverse(bf16[1,128,1536]{2,1,0:T(8,128)(2,1)} %collective-permute-done.3), dimensions={2} | reverse | bytes 786432 | tf_op jit(solution)/shard_map/rev | solution.py:25
  140.1 2.2 %fusion.90 = bf16[128,768]{1,0:T(8,128)(2,1)S(1)} fusion(f32[128,768]{1,0:T(8,128)S(1)} %fusion.11, f32[128,768]{1,0:T(8,128)S(1)} %fusion.17, f32[128,768]{1,0:T(8,128)S(1)} %fusion.25, f32[128,768]{1,0:T(8,128)S(1)} %fusion.33, bf16[5,1536,768]{2,1,0:T(8,128)(2,1)} %param.6, bf16[1,128,1536]{2,1,0:T(8,128)(2,1)S(1)} %rev.32), kind=kOutput, calls=%fused_computation.76 | convolution fusion | flops 302481408 | bytes 4521984 | tf_op jit(solution)/shard_map/dot_general | solution.py:54
  142.2 0.6 reverse.6
  142.9 2.3 %fusion.13 = f32[128,768]{1,0:T(8,128)S(1)} fusion(bf16[5,1536,768]{2,1,0:T(8,128)(2,1)} %param.6, bf16[1,128,1536]{2,1,0:T(8,128)(2,1)} %collective-permute-done.3), kind=kOutput, calls=%fused_computation.17 | convolution fusion | flops 301989888 | bytes 3145728 | tf_op jit(solution)/shard_map/dot_general | solution.py:54
  145.2 2.3 %fusion.19 = f32[128,768]{1,0:T(8,128)S(1)} fusion(bf16[5,1536,768]{2,1,0:T(8,128)(2,1)} %param.6, bf16[1,128,1536]{2,1,0:T(8,128)(2,1)} %collective-permute-done.2), kind=kOutput, calls=%fused_computation.23 | convolution fusion | flops 301989888 | bytes 3145728 | tf_op jit(solution)/shard_map/dot_general | solution.py:54
  147.5 2.1 %fusion.35 = f32[128,768]{1,0:T(8,128)S(1)} fusion(bf16[5,1536,768]{2,1,0:T(8,128)(2,1)} %param.6, bf16[1,128,1536]{2,1,0:T(8,128)(2,1)S(1)} %collective-permute-done.1), kind=kOutput, calls=%fused_computation.39 | convolution fusion | flops 301989888 | bytes 3145728 | tf_op jit(solution)/shard_map/dot_general | solution.py:54
  149.6 2.9 %fusion.96 = bf16[1,128,768]{2,1,0:T(8,128)(2,1)} fusion(f32[128,768]{1,0:T(8,128)S(1)} %fusion.13, f32[128,768]{1,0:T(8,128)S(1)} %fusion.19, f32[128,768]{1,0:T(8,128)S(1)} %fusion.27, f32[128,768]{1,0:T(8,128)S(1)} %fusion.35, bf16[5,1536,768]{2,1,0:T(8,128)(2,1)} %param.6, bf16[1,128,1536]{2,1,0:T(8,128)(2,1)S(1)} %collective-permute-done, ...), kind=kOutput, calls=%fused_computation.78 | convolution fusion | flops 302678016 | bytes 4718592 | tf_op jit(solution)/shard_map/dot_general | solution.py:54
  (18 shorter events, 0.1 us)
Async XLA Ops:
  0.6 20.1 %collective-permute-start.6 = (bf16[1,128,768]{2,1,0:T(8,128)(2,1)}, bf16[1,128,768]{2,1,0:T(8,128)(2,1)S(1)}, u32[]{:S(2)}, u32[]{:S(2)}) collective-permute-start(bf16[1,128,768]{2,1,0:T(8,128)(2,1)} %param.7), channel_id=1, source_target_pairs={{0,2},{1,3},{2,4},{3,5},{4,6},{5,7},{6,8},{7,9},{8,10},{9,11},{10,... | collective-permute-start | bytes 589832 | tf_op jit(solution)/shard_map/ppermute | solution.py:17
  5.5 18.4 %collective-permute-start.7 = (bf16[1,128,768]{2,1,0:T(8,128)(2,1)}, bf16[1,128,768]{2,1,0:T(8,128)(2,1)S(1)}, u32[]{:S(2)}, u32[]{:S(2)}) collective-permute-start(bf16[1,128,768]{2,1,0:T(8,128)(2,1)} %param.7), channel_id=1, source_target_pairs={{0,4},{1,5},{2,6},{3,7},{4,8},{5,9},{6,10},{7,11},{8,12},{9,13},{1... | collective-permute-start | bytes 589832 | tf_op jit(solution)/shard_map/ppermute | solution.py:17
  9.0 20.5 %collective-permute-start.4 = (bf16[1,128,768]{2,1,0:T(8,128)(2,1)}, bf16[1,128,768]{2,1,0:T(8,128)(2,1)}, u32[]{:S(2)}, u32[]{:S(2)}) collective-permute-start(bf16[1,128,768]{2,1,0:T(8,128)(2,1)} %param.7), channel_id=1, source_target_pairs={{4,0},{5,1},{6,2},{7,3},{8,4},{9,5},{10,6},{11,7},{12,8},{13,9},{1... | collective-permute-start | bytes 589832 | tf_op jit(solution)/shard_map/ppermute | solution.py:17
  10.3 24.5 %collective-permute-start.5 = (bf16[1,128,768]{2,1,0:T(8,128)(2,1)}, bf16[1,128,768]{2,1,0:T(8,128)(2,1)}, u32[]{:S(2)}, u32[]{:S(2)}) collective-permute-start(bf16[1,128,768]{2,1,0:T(8,128)(2,1)} %param.7), channel_id=1, source_target_pairs={{2,0},{3,1},{4,2},{5,3},{6,4},{7,5},{8,6},{9,7},{10,8},{11,9},{12,... | collective-permute-start | bytes 589832 | tf_op jit(solution)/shard_map/ppermute | solution.py:17
  20.7 3.2 %copy-start.3 = (bf16[1,128,768]{2,1,0:T(8,128)(2,1)}, bf16[1,128,768]{2,1,0:T(8,128)(2,1)S(1)}, u32[]{:S(2)}) copy-start(bf16[1,128,768]{2,1,0:T(8,128)(2,1)S(1)} %collective-permute-done.6) | copy-start | bytes 589828
  23.9 0.7 copy-start.1
  26.8 22.4 %copy-start = (bf16[1,128,1536]{2,1,0:T(8,128)(2,1)S(1)}, bf16[1,128,1536]{2,1,0:T(8,128)(2,1)}, u32[]{:S(2)}) copy-start(bf16[1,128,1536]{2,1,0:T(8,128)(2,1)} %param.4) | copy-start | bytes 1179652
  26.8 22.4 %copy-start.5 = (f32[1536]{0:T(1024)S(1)}, f32[1536]{0:T(1024)}, u32[]{:S(2)}) copy-start(f32[1536]{0:T(1024)} %param.5) | copy-start | bytes 18436
  29.6 14.4 %copy-start.2 = (bf16[1,128,768]{2,1,0:T(8,128)(2,1)S(1)}, bf16[1,128,768]{2,1,0:T(8,128)(2,1)}, u32[]{:S(2)}) copy-start(bf16[1,128,768]{2,1,0:T(8,128)(2,1)} %copy-done.1) | copy-start | bytes 589828
  40.1 9.2 %copy-start.4 = (bf16[1,128,768]{2,1,0:T(8,128)(2,1)S(1)}, bf16[1,128,768]{2,1,0:T(8,128)(2,1)}, u32[]{:S(2)}) copy-start(bf16[1,128,768]{2,1,0:T(8,128)(2,1)} %copy-done.3) | copy-start | bytes 589828
  53.7 65.4 %collective-permute-start = (bf16[1,128,1536]{2,1,0:T(8,128)(2,1)S(1)}, bf16[1,128,1536]{2,1,0:T(8,128)(2,1)S(1)}, u32[]{:S(2)}, u32[]{:S(2)}) collective-permute-start(bf16[1,128,1536]{2,1,0:T(8,128)(2,1)S(1)} %get-tuple-element.6), channel_id=1, source_target_pairs={{0,4},{1,5},{2,6},{3,7},{4,8},{5,9},{6,10},{7,11},{8,12},{9,13},{1... | collective-permute-start | bytes 1179656 | tf_op jit(solution)/shard_map/ppermute | solution.py:17
  59.2 63.3 %collective-permute-start.1 = (bf16[1,128,1536]{2,1,0:T(8,128)(2,1)S(1)}, bf16[1,128,1536]{2,1,0:T(8,128)(2,1)S(1)}, u32[]{:S(2)}, u32[]{:S(2)}) collective-permute-start(bf16[1,128,1536]{2,1,0:T(8,128)(2,1)S(1)} %get-tuple-element.6), channel_id=1, source_target_pairs={{0,2},{1,3},{2,4},{3,5},{4,6},{5,7},{6,8},{7,9},{8,10},{9,11},{10,... | collective-permute-start | bytes 1179656 | tf_op jit(solution)/shard_map/ppermute | solution.py:17
  62.8 63.0 %collective-permute-start.2 = (bf16[1,128,1536]{2,1,0:T(8,128)(2,1)S(1)}, bf16[1,128,1536]{2,1,0:T(8,128)(2,1)}, u32[]{:S(2)}, u32[]{:S(2)}) collective-permute-start(bf16[1,128,1536]{2,1,0:T(8,128)(2,1)S(1)} %get-tuple-element.6), channel_id=1, source_target_pairs={{2,0},{3,1},{4,2},{5,3},{6,4},{7,5},{8,6},{9,7},{10,8},{11,9},{12,... | collective-permute-start | bytes 1179656 | tf_op jit(solution)/shard_map/ppermute | solution.py:17
  64.1 70.7 %collective-permute-start.3 = (bf16[1,128,1536]{2,1,0:T(8,128)(2,1)S(1)}, bf16[1,128,1536]{2,1,0:T(8,128)(2,1)}, u32[]{:S(2)}, u32[]{:S(2)}) collective-permute-start(bf16[1,128,1536]{2,1,0:T(8,128)(2,1)S(1)} %get-tuple-element.6), channel_id=1, source_target_pairs={{4,0},{5,1},{6,2},{7,3},{8,4},{9,5},{10,6},{11,7},{12,8},{13,9},{1... | collective-permute-start | bytes 1179656 | tf_op jit(solution)/shard_map/ppermute | solution.py:17
where the time goes:
time: 155 us; the launch traced here: 153 us
  matrix products  49.2 us (32%)
  blocking collectives  47.5 us (31%)
  local copies, waits for them, and re-layouts  28.9 us (19%)
  starting transfers between devices  22.7 us (15%)
  other arithmetic  3.03 us (2%)
    psum x1, blocking collectives, per_device(): summed = lax.psum(partial_sum, ('dp', 'ctx'))  47.5 us
    dot_general x10, matrix products, apply_backward(): lax.dot_general(flat_rows, weight[tap_index], (((1,), (1,)), ((), ())), p...  26.6 us
    rev x10, local copies, waits for them, and re-layouts, flip_channels(): return values[:, :, ::-1]  26.4 us
    ppermute x8, starting transfers between devices, shifted(): return lax.ppermute(block, axis, route)  22.7 us
    dot_general x10, matrix products, apply_forward(): jnp.dot(flat_rows, weight[tap_index], preferred_element_type=jnp.float32)  22.6 us
  transfers between devices with their start and end apart: 8, of which 0 were waited for; matrix products, arithmetic and copies ran while one was open for 29% of the time, Pallas kernels for 0%

commit v1 on v0

v1 whole, which is shorter than its diff:
```python
import functools
import math

import jax
import jax.numpy as jnp
from jax import lax
from jax.experimental import pallas as pl
from jax.experimental.pallas import tpu as pltpu
from jax.sharding import PartitionSpec as P

TAPS = 5
MID = TAPS // 2
EPS = 1e-06
TILE = 256
CHUNK = 16
ROOT = math.sqrt(2.0 / math.pi)
CUBE = 0.044715
MESH = pl.DeviceIdType.MESH
ORDER = (0, 4, 1, 3, 2)


def body(n_dp, n_ctx, rows_total, feat, gain_ref, w, ct, conv_out, grad_out, gain_out,
         wv, xv, hh, fa, fb, csend, crecv, gg, bf, br, flip_ref, inv_ref, part, sum1, sum2,
         w_sem, x_sem, g_sem, ct_ssem, ct_rsem, c_ssem, c_rsem, s1_ssem, s1_rsem, s2_ssem, s2_rsem):
    rows, ch = xv.shape
    cout = ct.shape[-1]
    hops = n_ctx // 8
    low = 4 if n_ctx % 4 == 0 else 1
    high = n_ctx // low
    me_dp = lax.axis_index("dp")
    me = lax.axis_index("ctx")
    me_low = lax.rem(me, low)
    me_high = me // low
    group1 = n_dp * low
    slot1 = me_dp * low + me_low

    copies_w = {}
    x_copy = pltpu.make_async_copy(feat.at[0], xv, x_sem)
    x_copy.start()
    for k in ORDER:
        copies_w[k] = pltpu.make_async_copy(w.at[k], wv.at[k], w_sem.at[k])
        copies_w[k].start()
    g_copy = pltpu.make_async_copy(ct.at[0], gg.at[MID, pl.ds(0, rows)], g_sem)
    g_copy.start()

    def shifted(k):
        return me + (k - MID) * hops

    def exists(k):
        return jnp.logical_and(shifted(k) >= 0, shifted(k) < n_ctx)

    sides = [k for k in range(TAPS) if k != MID]
    far_first = (0, 4, 1, 3)

    def peer1(j):
        other = lax.rem(slot1 + j, group1)
        return {"dp": other // low, "ctx": me_high * low + lax.rem(other, low)}

    def peer2(j):
        other = lax.rem(me_high + j, high)
        return {"dp": me_dp, "ctx": other * low + me_low}

    barrier = pltpu.get_barrier_semaphore()
    count = jnp.int32(group1 - 1 + high - 1)
    for k in sides:
        @pl.when(exists(k))
        def _(k=k):
            pl.semaphore_signal(barrier, inc=1, device_id={"dp": me_dp, "ctx": shifted(k)}, device_id_type=MESH)
        count = count + exists(k).astype(jnp.int32)
    for j in range(1, group1):
        pl.semaphore_signal(barrier, inc=1, device_id=peer1(j), device_id_type=MESH)
    for j in range(1, high):
        pl.semaphore_signal(barrier, inc=1, device_id=peer2(j), device_id_type=MESH)
    pl.semaphore_wait(barrier, count)

    def ct_copy(k):
        return pltpu.make_async_remote_copy(
            src_ref=ct.at[0], dst_ref=gg.at[k, pl.ds(0, rows)],
            send_sem=ct_ssem.at[k], recv_sem=ct_rsem.at[k],
            device_id={"dp": me_dp, "ctx": shifted(k)}, device_id_type=MESH)

    def c_copy(k):
        return pltpu.make_async_remote_copy(
            src_ref=csend.at[k], dst_ref=crecv.at[k],
            send_sem=c_ssem.at[k], recv_sem=c_rsem.at[k],
            device_id={"dp": me_dp, "ctx": shifted(TAPS - 1 - k)}, device_id_type=MESH)

    for k in far_first:
        @pl.when(exists(k))
        def _(k=k):
            ct_copy(k).start()

    for k in sides:
        @pl.when(jnp.logical_not(exists(TAPS - 1 - k)))
        def _(k=k):
            gg[k, pl.ds(0, rows), :] = jnp.zeros((rows, cout), jnp.bfloat16)
        @pl.when(jnp.logical_not(exists(k)))
        def _(k=k):
            crecv[k] = jnp.zeros((rows, cout), jnp.bfloat16)

    r_iota = lax.broadcasted_iota(jnp.int32, (TILE, TILE), 0)
    c_iota = lax.broadcasted_iota(jnp.int32, (TILE, TILE), 1)
    flip_ref[...] = jnp.where(r_iota + c_iota == TILE - 1, 1.0, 0.0).astype(jnp.bfloat16)

    def flip_block(values):
        return jnp.dot(values, flip_ref[...], preferred_element_type=jnp.float32)

    def at(j):
        return pl.ds(pl.multiple_of(j * TILE, TILE), TILE)

    x_copy.wait()

    @pl.loop(0, rows // CHUNK)
    def _(i):
        here = pl.ds(pl.multiple_of(i * CHUNK, CHUNK), CHUNK)
        wide = xv[here, :].astype(jnp.float32)
        inv = lax.rsqrt(jnp.mean(wide * wide, axis=-1, keepdims=True) + EPS)
        inv_ref[here, :] = inv
        v = wide * inv * gain_ref[...]
        t = jnp.tanh(ROOT * (v + CUBE * (v * v * v)))
        hh[here, :] = (0.5 * v * (1.0 + t)).astype(jnp.bfloat16)

    @pl.loop(0, ch // TILE)
    def _(j):
        hh[pl.ds(rows, rows), at(ch // TILE - 1 - j)] = flip_block(hh[pl.ds(0, rows), at(j)]).astype(jnp.bfloat16)

    def forward(k):
        copies_w[k].wait()

        @pl.loop(0, cout // TILE)
        def _(j):
            res = jnp.dot(hh[...], wv[k, :, at(j)], preferred_element_type=jnp.float32)
            fa[k, :, at(j)] = res[:rows]
            fb[k, :, at(j)] = res[rows:].astype(jnp.bfloat16)

    def join(k):
        @pl.loop(0, cout // TILE)
        def _(j):
            csend[k, :, at(j)] = (
                fa[k, :, at(j)] + flip_block(fb[TAPS - 1 - k, :, at(cout // TILE - 1 - j)])
            ).astype(jnp.bfloat16)

        @pl.when(exists(TAPS - 1 - k))
        def _():
            c_copy(k).start()

    forward(0)
    forward(4)
    join(0)
    join(4)
    forward(1)
    forward(3)
    join(1)
    join(3)
    forward(2)

    g_copy.wait()
    for k in sides:
        @pl.when(exists(TAPS - 1 - k))
        def _(k=k):
            ct_copy(k).wait_recv()

    for k in range(TAPS):
        @pl.loop(0, cout // TILE)
        def _(j, k=k):
            gg[TAPS - 1 - k, pl.ds(rows, rows), at(cout // TILE - 1 - j)] = flip_block(
                gg[k, pl.ds(0, rows), at(j)]).astype(jnp.bfloat16)

    @pl.loop(0, ch // TILE)
    def _(j):
        total = jnp.zeros((2 * rows, TILE), jnp.float32)
        for k in range(TAPS):
            total = total + lax.dot_general(
                gg[k], wv[k, at(j), :], (((1,), (1,)), ((), ())), preferred_element_type=jnp.float32)
        bf[:, at(j)] = total[:rows]
        br[:, at(j)] = total[rows:].astype(jnp.bfloat16)

    @pl.loop(0, ch // TILE)
    def _(j):
        bf[:, at(j)] = bf[:, at(j)] + flip_block(br[:, at(ch // TILE - 1 - j)])

    part[...] = jnp.zeros_like(part)

    @pl.loop(0, rows // CHUNK)
    def _(i):
        here = pl.ds(pl.multiple_of(i * CHUNK, CHUNK), CHUNK)
        gain = gain_ref[...]
        inv = inv_ref[here, :]
        normed = xv[here, :].astype(jnp.float32) * inv
        v = normed * gain
        t = jnp.tanh(ROOT * (v + CUBE * (v * v * v)))
        slope = 0.5 * (1.0 + t) + 0.5 * v * (1.0 - t * t) * (ROOT * (1.0 + 3.0 * CUBE * (v * v)))
        product = bf[here, :] * slope
        mixed = product * normed
        part[...] += mixed[:8] + mixed[8:]
        spread = jnp.mean(mixed * gain, axis=-1, keepdims=True)
        grad_out[0, here, :] = (inv * (product * gain - normed * spread)).astype(jnp.bfloat16)

    sum1[slot1] = jnp.sum(part[...], axis=0, keepdims=True)

    def s1_copy(j):
        return pltpu.make_async_remote_copy(
            src_ref=sum1.at[slot1], dst_ref=sum1.at[slot1],
            send_sem=s1_ssem.at[j], recv_sem=s1_rsem.at[j],
            device_id=peer1(j), device_id_type=MESH)

    def s1_arrival(j):
        sender = lax.rem(slot1 + group1 - j, group1)
        return pltpu.make_async_remote_copy(
            src_ref=sum1.at[sender], dst_ref=sum1.at[sender],
            send_sem=s1_ssem.at[j], recv_sem=s1_rsem.at[j],
            device_id=peer1(j), device_id_type=MESH)

    for j in range(1, group1):
        s1_copy(j).start()
    for j in range(1, group1):
        s1_arrival(j).wait_recv()
    sum2[me_high] = jnp.sum(sum1[...], axis=0)

    def s2_copy(j):
        return pltpu.make_async_remote_copy(
            src_ref=sum2.at[me_high], dst_ref=sum2.at[me_high],
            send_sem=s2_ssem.at[j], recv_sem=s2_rsem.at[j],
            device_id=peer2(j), device_id_type=MESH)

    def s2_arrival(j):
        sender = lax.rem(me_high + high - j, high)
        return pltpu.make_async_remote_copy(
            src_ref=sum2.at[sender], dst_ref=sum2.at[sender],
            send_sem=s2_ssem.at[j], recv_sem=s2_rsem.at[j],
            device_id=peer2(j), device_id_type=MESH)

    for j in range(1, high):
        s2_copy(j).start()

    for k in sides:
        @pl.when(exists(k))
        def _(k=k):
            c_copy(k).wait_recv()

    @pl.loop(0, cout // TILE)
    def _(j):
        total = fa[MID, :, at(j)] + flip_block(fb[MID, :, at(cout // TILE - 1 - j)])
        for k in sides:
            total = total + crecv[k, :, at(j)].astype(jnp.float32)
        conv_out[0, :, at(j)] = total.astype(jnp.bfloat16)

    for j in range(1, high):
        s2_arrival(j).wait_recv()
    gain_out[...] = jnp.sum(sum2[...], axis=0) * (1.0 / math.sqrt(rows_total))

    for k in sides:
        @pl.when(exists(k))
        def _(k=k):
            ct_copy(k).wait_send()
        @pl.when(exists(TAPS - 1 - k))
        def _(k=k):
            c_copy(k).wait_send()
    for j in range(1, group1):
        s1_copy(j).wait_send()
    for j in range(1, high):
        s2_copy(j).wait_send()


def per_device(features, gain, conv_weight, cotangent):
    n_dp, n_ctx = lax.axis_size("dp"), lax.axis_size("ctx")
    lead, rows, ch = features.shape
    cout = cotangent.shape[-1]
    low = 4 if n_ctx % 4 == 0 else 1
    high = n_ctx // low
    group1 = n_dp * low
    rows_total = lead * rows * n_dp * n_ctx
    any_spec = pl.BlockSpec(memory_space=pl.ANY)
    vmem_spec = pl.BlockSpec(memory_space=pltpu.VMEM)
    bf16, f32 = jnp.bfloat16, jnp.float32
    dma = pltpu.SemaphoreType.DMA
    conv, grad, total = pl.pallas_call(
        functools.partial(body, n_dp, n_ctx, rows_total),
        out_shape=(
            jax.ShapeDtypeStruct((lead, rows, cout), bf16),
            jax.ShapeDtypeStruct((lead, rows, ch), bf16),
            jax.ShapeDtypeStruct((1, ch), f32),
        ),
        in_specs=[any_spec, vmem_spec, any_spec, any_spec],
        out_specs=(vmem_spec, vmem_spec, vmem_spec),
        scratch_shapes=[
            pltpu.VMEM((TAPS, ch, cout), bf16),
            pltpu.VMEM((rows, ch), bf16),
            pltpu.VMEM((2 * rows, ch), bf16),
            pltpu.VMEM((TAPS, rows, cout), f32),
            pltpu.VMEM((TAPS, rows, cout), bf16),
            pltpu.VMEM((TAPS, rows, cout), bf16),
            pltpu.VMEM((TAPS, rows, cout), bf16),
            pltpu.VMEM((TAPS, 2 * rows, cout), bf16),
            pltpu.VMEM((rows, ch), f32),
            pltpu.VMEM((rows, ch), bf16),
            pltpu.VMEM((TILE, TILE), bf16),
            pltpu.VMEM((rows, 1), f32),
            pltpu.VMEM((8, ch), f32),
            pltpu.VMEM((group1, 1, ch), f32),
            pltpu.VMEM((high, 1, ch), f32),
            dma((TAPS,)), dma, dma,
            dma((TAPS,)), dma((TAPS,)), dma((TAPS,)), dma((TAPS,)),
            dma((group1,)), dma((group1,)), dma((high,)), dma((high,)),
        ],
        compiler_params=pltpu.CompilerParams(
            collective_id=0, has_side_effects=True, vmem_limit_bytes=62 * 1024 * 1024),
        name="rc_block",
    )(features, gain.reshape(1, ch), conv_weight, cotangent)
    return conv, grad, total.reshape(ch)


def solution(mesh):
    return jax.shard_map(
        per_device,
        mesh=mesh,
        in_specs=(P("dp", "ctx", None), P(), P(), P("dp", "ctx", None)),
        out_specs=(P("dp", "ctx", None), P("dp", "ctx", None), P()),
        check_vma=False,
    )
```

time: 155 us -> 43 us (0.28); the launches traced: 153 us -> 42.6 us
  matrix products: 49.2 us -> 0 us
  blocking collectives: 47.5 us -> 0 us
  Pallas kernels: 0 us -> 36 us
  local copies, waits for them, and re-layouts: 28.9 us -> 4.68 us
  starting transfers between devices: 22.7 us -> 0 us
  other arithmetic: 3.03 us -> 1.31 us
    dot_general x20 -> x0, matrix products: 49.2 us -> none  [the longest x10 26.6 us: apply_backward(): lax.dot_general(flat_rows, weight[tap_index], (((1,), (1,)), ((), ())), p...]
    psum x1 -> x0, blocking collectives: 47.5 us -> none  [per_device(): summed = lax.psum(partial_sum, ('dp', 'ctx'))]
    pallas_call x0 -> x1, Pallas kernels: none -> 36 us  [per_device(): pl.pallas_call(functools.partial(body, n_dp, n_ctx, rows_total), out_shap...]
    rev x10 -> x0, local copies, waits for them, and re-layouts: 26.4 us -> none  [flip_channels(): return values[:, :, ::-1]]
    ppermute x8 -> x0, starting transfers between devices: 22.7 us -> none  [shifted(): return lax.ppermute(block, axis, route)]
    unnamed x12 -> x2, local copies, waits for them, and re-layouts: 0.69 us -> 3.38 us
    another operation x2 -> x0, local copies, waits for them, and re-layouts: 1.84 us -> none
  transfers between devices with their start and end apart: 8 -> 0, of which waited for: 0 -> 0; matrix products, arithmetic and copies ran while one was open for 29% -> 0% of each run, Pallas kernels for 0% -> 0%
where the time goes in v1:
time: 43 us; the launch traced here: 42.6 us
  Pallas kernels  36 us (84%)
  local copies, waits for them, and re-layouts  4.68 us (11%)
  other arithmetic  1.31 us (3%)
  between operations  0.64 us (1%)
    pallas_call x1, Pallas kernels, per_device(): pl.pallas_call(functools.partial(body, n_dp, n_ctx, rows_total), out_shap...  36 us
    unnamed x2, local copies, waits for them, and re-layouts  3.38 us
    pallas_call x1, other arithmetic, per_device(): pl.pallas_call(functools.partial(body, n_dp, n_ctx, rows_total), out_shap...  1.31 us
    reshape x1, local copies, waits for them, and re-layouts, per_device(): gain.reshape(1, ch)  1.3 us

profile of v1, /device:TPU:0, one launch (start us, length us, event | category | flops | bytes accessed | tf_op | source)
XLA Modules:
  0.0 42.6 jit_solution(5271377342708292648)
XLA Ops:
  0.6 1.3 %reshape.12.gain_ref = f32[1,1536]{1,0:T(1,128)} reshape(f32[1536]{0:T(1024)} %param.5) | data formatting | bytes 12288 | tf_op jit(solution)/shard_map/reshape | solution.py:309
  1.9 36.0 %rc_block.1 = (bf16[1,128,768]{2,1,0:T(8,128)(2,1)}, bf16[1,128,1536]{2,1,0:T(8,128)(2,1)}, f32[1,1536]{1,0:T(1,128)}) custom-call(bf16[1,128,1536]{2,1,0:T(8,128)(2,1)} %feat.1, f32[1,1536]{1,0:T(1,128)} %reshape.12.gain_ref, bf16[5,1536,768]{2,1,0:T(8,128)(2,1)} %w.1, bf16[1,128,768]{2,1,0:T(8,128)(2,1)} %ct.1), custom_call_target="tpu_custom_call" | custom-call | tf_op jit(solution)/shard_map/rc_block/pallas_call | solution.py:277
  38.0 1.3 %reduce = f32[1536]{0:T(1024)} reduce(f32[1,1536]{1,0:T(1,128)} %get-tuple-element.8, f32[]{:T(128)} %constant.2), dimensions={0}, to_apply=%get-tuple-element.8.reduce_sub_computation | reduce | bytes 12292 | tf_op jit(solution)/shard_map/rc_block/pallas_call | solution.py:277
  39.3 1.6 %copy.9 = bf16[1,128,768]{2,1,0:T(8,128)(2,1)} copy(bf16[1,128,768]{2,1,0:T(8,128)(2,1)} %get-tuple-element.12) | data formatting | bytes 393216
  40.9 1.8 %copy.10 = bf16[1,128,1536]{2,1,0:T(8,128)(2,1)} copy(bf16[1,128,1536]{2,1,0:T(8,128)(2,1)} %get-tuple-element.13) | data formatting | bytes 786432

commit v2 on v1

--- a/solution.py
+++ b/solution.py
@@ -19,8 +19,8 @@
 ORDER = (0, 4, 1, 3, 2)
 
 
-def body(n_dp, n_ctx, rows_total, feat, gain_ref, w, ct, conv_out, grad_out, gain_out,
-         wv, xv, hh, fa, fb, csend, crecv, gg, bf, br, flip_ref, inv_ref, part, sum1, sum2,
+def body(n_dp, n_ctx, rows_total, feat, gain_in, w, ct, conv_out, grad_out, gain_out,
+         gain_ref, wv, xv, hh, fa, fb, csend, crecv, gg, bf, br, flip_ref, inv_ref, spread_ref, part, sum1, sum2,
          w_sem, x_sem, g_sem, ct_ssem, ct_rsem, c_ssem, c_rsem, s1_ssem, s1_rsem, s2_ssem, s2_rsem):
     rows, ch = xv.shape
     cout = ct.shape[-1]
@@ -108,6 +108,16 @@
     def at(j):
         return pl.ds(pl.multiple_of(j * TILE, TILE), TILE)
 
+    def flip_all(blocks):
+        turned = flip_block(jnp.concatenate(blocks[::-1], axis=0))
+        return [turned[n * rows:(n + 1) * rows] for n in range(len(blocks))]
+
+    n_out, n_in = cout // TILE, ch // TILE
+    top, bottom = pl.ds(0, rows), pl.ds(rows, rows)
+    tile = [pl.ds(j * TILE, TILE) for j in range(max(n_out, n_in))]
+
+    gain_ref[...] = gain_in[...].reshape(1, ch)
+
     x_copy.wait()
 
     @pl.loop(0, rows // CHUNK)
@@ -120,13 +130,10 @@
         t = jnp.tanh(ROOT * (v + CUBE * (v * v * v)))
         hh[here, :] = (0.5 * v * (1.0 + t)).astype(jnp.bfloat16)
 
-    @pl.loop(0, ch // TILE)
-    def _(j):
-        hh[pl.ds(rows, rows), at(ch // TILE - 1 - j)] = flip_block(hh[pl.ds(0, rows), at(j)]).astype(jnp.bfloat16)
+    for j, block in enumerate(flip_all([hh[top, tile[j]] for j in range(n_in)])):
+        hh[bottom, tile[j]] = block.astype(jnp.bfloat16)
 
     def forward(k):
-        copies_w[k].wait()
-
         @pl.loop(0, cout // TILE)
         def _(j):
             res = jnp.dot(hh[...], wv[k, :, at(j)], preferred_element_type=jnp.float32)
@@ -134,25 +141,24 @@
             fb[k, :, at(j)] = res[rows:].astype(jnp.bfloat16)
 
     def join(k):
-        @pl.loop(0, cout // TILE)
-        def _(j):
-            csend[k, :, at(j)] = (
-                fa[k, :, at(j)] + flip_block(fb[TAPS - 1 - k, :, at(cout // TILE - 1 - j)])
-            ).astype(jnp.bfloat16)
+        for j, block in enumerate(flip_all([fb[TAPS - 1 - k, :, tile[j]] for j in range(n_out)])):
+            csend[k, :, tile[j]] = (fa[k, :, tile[j]] + block).astype(jnp.bfloat16)
 
         @pl.when(exists(TAPS - 1 - k))
         def _():
             c_copy(k).start()
 
-    forward(0)
-    forward(4)
+    for k in (0, 4):
+        copies_w[k].wait()
+        forward(k)
     join(0)
     join(4)
-    forward(1)
-    forward(3)
+    for k in (1, 3):
+        copies_w[k].wait()
+        forward(k)
     join(1)
     join(3)
-    forward(2)
+    copies_w[MID].wait()
 
     g_copy.wait()
     for k in sides:
@@ -161,10 +167,8 @@
             ct_copy(k).wait_recv()
 
     for k in range(TAPS):
-        @pl.loop(0, cout // TILE)
-        def _(j, k=k):
-            gg[TAPS - 1 - k, pl.ds(rows, rows), at(cout // TILE - 1 - j)] = flip_block(
-                gg[k, pl.ds(0, rows), at(j)]).astype(jnp.bfloat16)
+        for j, block in enumerate(flip_all([gg[k, top, tile[j]] for j in range(n_out)])):
+            gg[TAPS - 1 - k, bottom, tile[j]] = block.astype(jnp.bfloat16)
 
     @pl.loop(0, ch // TILE)
     def _(j):
@@ -175,9 +179,8 @@
         bf[:, at(j)] = total[:rows]
         br[:, at(j)] = total[rows:].astype(jnp.bfloat16)
 
-    @pl.loop(0, ch // TILE)
-    def _(j):
-        bf[:, at(j)] = bf[:, at(j)] + flip_block(br[:, at(ch // TILE - 1 - j)])
+    for j, block in enumerate(flip_all([br[:, tile[j]] for j in range(n_in)])):
+        bf[:, tile[j]] = bf[:, tile[j]] + block
 
     part[...] = jnp.zeros_like(part)
 
@@ -193,8 +196,8 @@
         product = bf[here, :] * slope
         mixed = product * normed
         part[...] += mixed[:8] + mixed[8:]
-        spread = jnp.mean(mixed * gain, axis=-1, keepdims=True)
-        grad_out[0, here, :] = (inv * (product * gain - normed * spread)).astype(jnp.bfloat16)
+        bf[here, :] = product * gain
+        spread_ref[here, :] = jnp.mean(mixed * gain, axis=-1, keepdims=True)
 
     sum1[slot1] = jnp.sum(part[...], axis=0, keepdims=True)
 
@@ -213,6 +216,7 @@
 
     for j in range(1, group1):
         s1_copy(j).start()
+    forward(2)
     for j in range(1, group1):
         s1_arrival(j).wait_recv()
     sum2[me_high] = jnp.sum(sum1[...], axis=0)
@@ -238,12 +242,18 @@
         def _(k=k):
             c_copy(k).wait_recv()
 
-    @pl.loop(0, cout // TILE)
-    def _(j):
-        total = fa[MID, :, at(j)] + flip_block(fb[MID, :, at(cout // TILE - 1 - j)])
+    for j, block in enumerate(flip_all([fb[MID, :, tile[j]] for j in range(n_out)])):
+        total = fa[MID, :, tile[j]] + block
         for k in sides:
-            total = total + crecv[k, :, at(j)].astype(jnp.float32)
-        conv_out[0, :, at(j)] = total.astype(jnp.bfloat16)
+            total = total + crecv[k, :, tile[j]].astype(jnp.float32)
+        conv_out[0, :, tile[j]] = total.astype(jnp.bfloat16)
+
+    @pl.loop(0, rows // CHUNK)
+    def _(i):
+        here = pl.ds(pl.multiple_of(i * CHUNK, CHUNK), CHUNK)
+        inv = inv_ref[here, :]
+        normed = xv[here, :].astype(jnp.float32) * inv
+        grad_out[0, here, :] = (inv * (bf[here, :] - normed * spread_ref[here, :])).astype(jnp.bfloat16)
 
     for j in range(1, high):
         s2_arrival(j).wait_recv()
@@ -260,6 +270,12 @@
         s1_copy(j).wait_send()
     for j in range(1, high):
         s2_copy(j).wait_send()
+
+
+def hand_over(conv, grad, total, conv_out, grad_out, total_out):
+    conv_out[...] = conv[...]
+    grad_out[...] = grad[...]
+    total_out[...] = total[...].reshape(total_out.shape)
 
 
 def per_device(features, gain, conv_weight, cotangent):
@@ -270,7 +286,7 @@
     high = n_ctx // low
     group1 = n_dp * low
     rows_total = lead * rows * n_dp * n_ctx
-    any_spec = pl.BlockSpec(memory_space=pl.ANY)
+    hbm_spec = pl.BlockSpec(memory_space=pltpu.HBM)
     vmem_spec = pl.BlockSpec(memory_space=pltpu.VMEM)
     bf16, f32 = jnp.bfloat16, jnp.float32
     dma = pltpu.SemaphoreType.DMA
@@ -281,9 +297,10 @@
             jax.ShapeDtypeStruct((lead, rows, ch), bf16),
             jax.ShapeDtypeStruct((1, ch), f32),
         ),
-        in_specs=[any_spec, vmem_spec, any_spec, any_spec],
+        in_specs=[hbm_spec, vmem_spec, hbm_spec, hbm_spec],
         out_specs=(vmem_spec, vmem_spec, vmem_spec),
         scratch_shapes=[
+            pltpu.VMEM((1, ch), f32),
             pltpu.VMEM((TAPS, ch, cout), bf16),
             pltpu.VMEM((rows, ch), bf16),
             pltpu.VMEM((2 * rows, ch), bf16),
@@ -296,6 +313,7 @@
             pltpu.VMEM((rows, ch), bf16),
             pltpu.VMEM((TILE, TILE), bf16),
             pltpu.VMEM((rows, 1), f32),
+            pltpu.VMEM((rows, 1), f32),
             pltpu.VMEM((8, ch), f32),
             pltpu.VMEM((group1, 1, ch), f32),
             pltpu.VMEM((high, 1, ch), f32),
@@ -304,10 +322,21 @@
             dma((group1,)), dma((group1,)), dma((high,)), dma((high,)),
         ],
         compiler_params=pltpu.CompilerParams(
-            collective_id=0, has_side_effects=True, vmem_limit_bytes=62 * 1024 * 1024),
+            collective_id=0, has_side_effects=True, vmem_limit_bytes=53_000_000),
         name="rc_block",
-    )(features, gain.reshape(1, ch), conv_weight, cotangent)
-    return conv, grad, total.reshape(ch)
+    )(features, gain, conv_weight, cotangent)
+    return pl.pallas_call(
+        hand_over,
+        out_shape=(
+            jax.ShapeDtypeStruct(conv.shape, bf16),
+            jax.ShapeDtypeStruct(grad.shape, bf16),
+            jax.ShapeDtypeStruct((ch,), f32),
+        ),
+        in_specs=[vmem_spec] * 3,
+        out_specs=(vmem_spec,) * 3,
+        compiler_params=pltpu.CompilerParams(vmem_limit_bytes=4 * 1024 * 1024),
+        name="hand_over",
+    )(conv, grad, total)
 
 
 def solution(mesh):

time: 43 us -> 35.3 us (0.82)
  Pallas kernels: 36 us -> 31.8 us
  local copies, waits for them, and re-layouts: 4.68 us -> 2.61 us
  other arithmetic: 1.31 us -> 0 us
    pallas_call x1, Pallas kernels: 36 us -> 31 us  [per_device(): pl.pallas_call(functools.partial(body, n_dp, n_ctx, rows_total), out_shap...]
    pallas_call x1 -> x0, other arithmetic: 1.31 us -> none  [per_device(): pl.pallas_call(functools.partial(body, n_dp, n_ctx, rows_total), out_shap...]
    reshape x1 -> x0, local copies, waits for them, and re-layouts: 1.3 us -> none  [per_device(): gain.reshape(1, ch)]
    pallas_call x0 -> x1, Pallas kernels: none -> 0.85 us  [per_device(): pl.pallas_call(hand_over, out_shape=(jax.ShapeDtypeStruct(conv.shape, bf1...]
    unnamed x2 -> x6, local copies, waits for them, and re-layouts: 3.38 us -> 2.61 us
where the time goes in v2:
time: 35.3 us; the launch traced here: 35.1 us
  Pallas kernels  31.8 us (90%)
  local copies, waits for them, and re-layouts  2.61 us (7%)
  between operations  0.65 us (2%)
    pallas_call x1, Pallas kernels, per_device(): pl.pallas_call(functools.partial(body, n_dp, n_ctx, rows_total), out_shap...  31 us
    unnamed x6, local copies, waits for them, and re-layouts  2.61 us
    pallas_call x1, Pallas kernels, per_device(): pl.pallas_call(hand_over, out_shape=(jax.ShapeDtypeStruct(conv.shape, bf1...  0.85 us

profile of v2, /device:TPU:0, one launch (start us, length us, event | category | flops | bytes accessed | tf_op | source)
XLA Modules:
  0.0 35.1 jit_solution(7525103838273095885)
XLA Ops:
  0.6 0.0 copy-start
  0.6 1.0 %copy-done = bf16[1,128,1536]{2,1,0:T(8,128)(2,1)S(1)} copy-done((bf16[1,128,1536]{2,1,0:T(8,128)(2,1)S(1)}, bf16[1,128,1536]{2,1,0:T(8,128)(2,1)}, u32[]{:S(2)}) %copy-start) | copy-done | bytes 393240
  1.6 0.0 copy-start.1
  1.6 0.9 %copy-done.1 = bf16[1,128,768]{2,1,0:T(8,128)(2,1)S(1)} copy-done((bf16[1,128,768]{2,1,0:T(8,128)(2,1)S(1)}, bf16[1,128,768]{2,1,0:T(8,128)(2,1)}, u32[]{:S(2)}) %copy-start.1) | copy-done | bytes 196632
  2.6 0.0 copy-start.2
  2.6 0.7 %copy-done.2 = f32[1536]{0:T(1024)S(1)} copy-done((f32[1536]{0:T(1024)S(1)}, f32[1536]{0:T(1024)}, u32[]{:S(2)}) %copy-start.2) | copy-done | bytes 6168
  3.3 31.0 %rc_block.1 = (bf16[1,128,768]{2,1,0:T(8,128)(2,1)S(1)}, bf16[1,128,1536]{2,1,0:T(8,128)(2,1)S(1)}, f32[1,1536]{1,0:T(1,128)S(1)}) custom-call(bf16[1,128,1536]{2,1,0:T(8,128)(2,1)S(1)} %copy-done, f32[1536]{0:T(1024)S(1)} %copy-done.2, bf16[5,1536,768]{2,1,0:T(8,128)(2,1)} %w.1, bf16[1,128,768]{2,1,0:T(8,128)(2,1)S(1)} %copy-done.1), custom_call_target="tpu_custom_call" | custom-call | tf_op jit(solution)/shard_map/rc_block/pallas_call | solution.py:293
  34.2 0.8 %hand_over.1 = (bf16[1,128,768]{2,1,0:T(8,128)(2,1)}, bf16[1,128,1536]{2,1,0:T(8,128)(2,1)}, f32[1536]{0:T(1024)}) custom-call(bf16[1,128,768]{2,1,0:T(8,128)(2,1)S(1)} %get-tuple-element.6.conv, bf16[1,128,1536]{2,1,0:T(8,128)(2,1)S(1)} %get-tuple-element.7.grad, f32[1,1536]{1,0:T(1,128)S(1)} %get-tuple-element.8.total), custom_call_target="tpu_custom_call" | custom-call | tf_op jit(solution)/shard_map/hand_over/pallas_call | solution.py:328
Async XLA Ops:
  0.6 1.0 %copy-start = (bf16[1,128,1536]{2,1,0:T(8,128)(2,1)S(1)}, bf16[1,128,1536]{2,1,0:T(8,128)(2,1)}, u32[]{:S(2)}) copy-start(bf16[1,128,1536]{2,1,0:T(8,128)(2,1)} %feat.1) | copy-start | bytes 1179652
  1.6 0.9 %copy-start.1 = (bf16[1,128,768]{2,1,0:T(8,128)(2,1)S(1)}, bf16[1,128,768]{2,1,0:T(8,128)(2,1)}, u32[]{:S(2)}) copy-start(bf16[1,128,768]{2,1,0:T(8,128)(2,1)} %ct.1) | copy-start | bytes 589828
  2.6 0.7 %copy-start.2 = (f32[1536]{0:T(1024)S(1)}, f32[1536]{0:T(1024)}, u32[]{:S(2)}) copy-start(f32[1536]{0:T(1024)} %gain_in.1) | copy-start | bytes 18436

commit v3 on v2

--- a/solution.py
+++ b/solution.py
@@ -20,8 +20,8 @@
 
 
 def body(n_dp, n_ctx, rows_total, feat, gain_in, w, ct, conv_out, grad_out, gain_out,
-         gain_ref, wv, xv, hh, fa, fb, csend, crecv, gg, bf, br, flip_ref, inv_ref, spread_ref, part, sum1, sum2,
-         w_sem, x_sem, g_sem, ct_ssem, ct_rsem, c_ssem, c_rsem, s1_ssem, s1_rsem, s2_ssem, s2_rsem):
+         gain_ref, gain_v, acc, wv, xv, hh, fa, fb, csend, crecv, gg, bf, br, flip_ref, inv_ref, spread_ref, part, sum1, sum2,
+         w_sem, x_sem, g_sem, v_sem, ct_ssem, ct_rsem, c_ssem, c_rsem, s1_ssem, s1_rsem, s2_ssem, s2_rsem):
     rows, ch = xv.shape
     cout = ct.shape[-1]
     hops = n_ctx // 8
@@ -37,6 +37,8 @@
     copies_w = {}
     x_copy = pltpu.make_async_copy(feat.at[0], xv, x_sem)
     x_copy.start()
+    v_copy = pltpu.make_async_copy(gain_in, gain_v, v_sem)
+    v_copy.start()
     for k in ORDER:
         copies_w[k] = pltpu.make_async_copy(w.at[k], wv.at[k], w_sem.at[k])
         copies_w[k].start()
@@ -50,7 +52,7 @@
         return jnp.logical_and(shifted(k) >= 0, shifted(k) < n_ctx)
 
     sides = [k for k in range(TAPS) if k != MID]
-    far_first = (0, 4, 1, 3)
+    near_first = (1, 3, 0, 4)
 
     def peer1(j):
         other = lax.rem(slot1 + j, group1)
@@ -85,7 +87,7 @@
             send_sem=c_ssem.at[k], recv_sem=c_rsem.at[k],
             device_id={"dp": me_dp, "ctx": shifted(TAPS - 1 - k)}, device_id_type=MESH)
 
-    for k in far_first:
+    for k in near_first:
         @pl.when(exists(k))
         def _(k=k):
             ct_copy(k).start()
@@ -116,7 +118,8 @@
     top, bottom = pl.ds(0, rows), pl.ds(rows, rows)
     tile = [pl.ds(j * TILE, TILE) for j in range(max(n_out, n_in))]
 
-    gain_ref[...] = gain_in[...].reshape(1, ch)
+    v_copy.wait()
+    gain_ref[...] = gain_v[...].reshape(1, ch)
 
     x_copy.wait()
 
@@ -144,6 +147,7 @@
         for j, block in enumerate(flip_all([fb[TAPS - 1 - k, :, tile[j]] for j in range(n_out)])):
             csend[k, :, tile[j]] = (fa[k, :, tile[j]] + block).astype(jnp.bfloat16)
 
+    def leave(k):
         @pl.when(exists(TAPS - 1 - k))
         def _():
             c_copy(k).start()
@@ -152,30 +156,44 @@
         copies_w[k].wait()
         forward(k)
     join(0)
+    leave(0)
     join(4)
+    leave(4)
     for k in (1, 3):
         copies_w[k].wait()
         forward(k)
     join(1)
+    leave(1)
     join(3)
     copies_w[MID].wait()
 
-    g_copy.wait()
-    for k in sides:
-        @pl.when(exists(TAPS - 1 - k))
-        def _(k=k):
-            ct_copy(k).wait_recv()
-
-    for k in range(TAPS):
+    def flip_tap(k):
         for j, block in enumerate(flip_all([gg[k, top, tile[j]] for j in range(n_out)])):
             gg[TAPS - 1 - k, bottom, tile[j]] = block.astype(jnp.bfloat16)
 
-    @pl.loop(0, ch // TILE)
+    def backward(k, j):
+        return lax.dot_general(
+            gg[k], wv[k, at(j), :], (((1,), (1,)), ((), ())), preferred_element_type=jnp.float32)
+
+    g_copy.wait()
+    flip_tap(MID)
+
+    @pl.loop(0, n_in)
     def _(j):
-        total = jnp.zeros((2 * rows, TILE), jnp.float32)
-        for k in range(TAPS):
-            total = total + lax.dot_general(
-                gg[k], wv[k, at(j), :], (((1,), (1,)), ((), ())), preferred_element_type=jnp.float32)
+        acc[:, at(j)] = backward(MID, j)
+
+    for k in sides:
+        @pl.when(exists(TAPS - 1 - k))
+        def _(k=k):
+            ct_copy(k).wait_recv()
+    for k in sides:
+        flip_tap(k)
+
+    @pl.loop(0, n_in)
+    def _(j):
+        total = acc[:, at(j)]
+        for k in sides:
+            total = total + backward(k, j)
         bf[:, at(j)] = total[:rows]
         br[:, at(j)] = total[rows:].astype(jnp.bfloat16)
 
@@ -216,6 +234,7 @@
 
     for j in range(1, group1):
         s1_copy(j).start()
+    leave(3)
     forward(2)
     for j in range(1, group1):
         s1_arrival(j).wait_recv()
@@ -297,10 +316,12 @@
             jax.ShapeDtypeStruct((lead, rows, ch), bf16),
             jax.ShapeDtypeStruct((1, ch), f32),
         ),
-        in_specs=[hbm_spec, vmem_spec, hbm_spec, hbm_spec],
+        in_specs=[hbm_spec] * 4,
         out_specs=(vmem_spec, vmem_spec, vmem_spec),
         scratch_shapes=[
             pltpu.VMEM((1, ch), f32),
+            pltpu.VMEM((ch,), f32),
+            pltpu.VMEM((2 * rows, ch), f32),
             pltpu.VMEM((TAPS, ch, cout), bf16),
             pltpu.VMEM((rows, ch), bf16),
             pltpu.VMEM((2 * rows, ch), bf16),
@@ -317,14 +338,14 @@
             pltpu.VMEM((8, ch), f32),
             pltpu.VMEM((group1, 1, ch), f32),
             pltpu.VMEM((high, 1, ch), f32),
-            dma((TAPS,)), dma, dma,
+            dma((TAPS,)), dma, dma, dma,
             dma((TAPS,)), dma((TAPS,)), dma((TAPS,)), dma((TAPS,)),
             dma((group1,)), dma((group1,)), dma((high,)), dma((high,)),
         ],
         compiler_params=pltpu.CompilerParams(
             collective_id=0, has_side_effects=True, vmem_limit_bytes=53_000_000),
         name="rc_block",
-    )(features, gain, conv_weight, cotangent)
+    )(*[pltpu.with_memory_space_constraint(x, pltpu.HBM) for x in (features, gain, conv_weight, cotangent)])
     return pl.pallas_call(
         hand_over,
         out_shape=(

time: 35.3 us -> 31.9 us (0.904)
  local copies, waits for them, and re-layouts: 2.61 us -> 0 us
  Pallas kernels: 31.8 us -> 31.1 us
    unnamed x6 -> x0, local copies, waits for them, and re-layouts: 2.61 us -> none
    pallas_call x1, Pallas kernels: 31 us -> 30.2 us  [per_device(): pl.pallas_call(functools.partial(body, n_dp, n_ctx, rows_total), out_shap...]
where the time goes in v3:
time: 31.9 us; the launch traced here: 31.7 us
  Pallas kernels  31.1 us (97%)
  between operations  0.64 us (2%)
    pallas_call x1, Pallas kernels, per_device(): pl.pallas_call(functools.partial(body, n_dp, n_ctx, rows_total), out_shap...  30.2 us
    pallas_call x1, Pallas kernels, per_device(): pl.pallas_call(hand_over, out_shape=(jax.ShapeDtypeStruct(conv.shape, bf1...  0.85 us

profile of v3, /device:TPU:0, one launch (start us, length us, event | category | flops | bytes accessed | tf_op | source)
XLA Modules:
  0.0 31.7 jit_solution(17377802286818053989)
XLA Ops:
  0.6 30.2 %rc_block.1 = (bf16[1,128,768]{2,1,0:T(8,128)(2,1)S(1)}, bf16[1,128,1536]{2,1,0:T(8,128)(2,1)S(1)}, f32[1,1536]{1,0:T(1,128)S(1)}) custom-call(bf16[1,128,1536]{2,1,0:T(8,128)(2,1)} %feat.1, f32[1536]{0:T(1024)} %gain_in.1, bf16[5,1536,768]{2,1,0:T(8,128)(2,1)} %w.1, bf16[1,128,768]{2,1,0:T(8,128)(2,1)} %ct.1), custom_call_target="tpu_custom_call" | custom-call | tf_op jit(solution)/shard_map/rc_block/pallas_call | solution.py:312
  30.9 0.8 %hand_over.1 = (bf16[1,128,768]{2,1,0:T(8,128)(2,1)}, bf16[1,128,1536]{2,1,0:T(8,128)(2,1)}, f32[1536]{0:T(1024)}) custom-call(bf16[1,128,768]{2,1,0:T(8,128)(2,1)S(1)} %get-tuple-element.6.conv, bf16[1,128,1536]{2,1,0:T(8,128)(2,1)S(1)} %get-tuple-element.7.grad, f32[1,1536]{1,0:T(1,128)S(1)} %get-tuple-element.8.total), custom_call_target="tpu_custom_call" | custom-call | tf_op jit(solution)/shard_map/hand_over/pallas_call | solution.py:349

commit v4 on v3

--- a/solution.py
+++ b/solution.py
@@ -123,7 +123,7 @@
 
     x_copy.wait()
 
-    @pl.loop(0, rows // CHUNK)
+    @pl.loop(0, rows // CHUNK, unroll=2)
     def _(i):
         here = pl.ds(pl.multiple_of(i * CHUNK, CHUNK), CHUNK)
         wide = xv[here, :].astype(jnp.float32)
@@ -137,7 +137,7 @@
         hh[bottom, tile[j]] = block.astype(jnp.bfloat16)
 
     def forward(k):
-        @pl.loop(0, cout // TILE)
+        @pl.loop(0, cout // TILE, unroll=True)
         def _(j):
             res = jnp.dot(hh[...], wv[k, :, at(j)], preferred_element_type=jnp.float32)
             fa[k, :, at(j)] = res[:rows]
@@ -178,7 +178,7 @@
     g_copy.wait()
     flip_tap(MID)
 
-    @pl.loop(0, n_in)
+    @pl.loop(0, n_in, unroll=2)
     def _(j):
         acc[:, at(j)] = backward(MID, j)
 
@@ -189,7 +189,7 @@
     for k in sides:
         flip_tap(k)
 
-    @pl.loop(0, n_in)
+    @pl.loop(0, n_in, unroll=2)
     def _(j):
         total = acc[:, at(j)]
         for k in sides:
@@ -202,7 +202,7 @@
 
     part[...] = jnp.zeros_like(part)
 
-    @pl.loop(0, rows // CHUNK)
+    @pl.loop(0, rows // CHUNK, unroll=2)
     def _(i):
         here = pl.ds(pl.multiple_of(i * CHUNK, CHUNK), CHUNK)
         gain = gain_ref[...]
@@ -267,7 +267,7 @@
             total = total + crecv[k, :, tile[j]].astype(jnp.float32)
         conv_out[0, :, tile[j]] = total.astype(jnp.bfloat16)
 
-    @pl.loop(0, rows // CHUNK)
+    @pl.loop(0, rows // CHUNK, unroll=2)
     def _(i):
         here = pl.ds(pl.multiple_of(i * CHUNK, CHUNK), CHUNK)
         inv = inv_ref[here, :]

time: 31.9 us -> 30.7 us (0.962)
  Pallas kernels: 31.1 us -> 29.9 us
    pallas_call x1, Pallas kernels: 30.2 us -> 29 us  [per_device(): pl.pallas_call(functools.partial(body, n_dp, n_ctx, rows_total), out_shap...]
where the time goes in v4:
time: 30.7 us; the launch traced here: 30.5 us
  Pallas kernels  29.9 us (97%)
  between operations  0.64 us (2%)
    pallas_call x1, Pallas kernels, per_device(): pl.pallas_call(functools.partial(body, n_dp, n_ctx, rows_total), out_shap...  29 us
    pallas_call x1, Pallas kernels, per_device(): pl.pallas_call(hand_over, out_shape=(jax.ShapeDtypeStruct(conv.shape, bf1...  0.85 us

profile of v4, /device:TPU:0, one launch (start us, length us, event | category | flops | bytes accessed | tf_op | source)
XLA Modules:
  0.0 30.5 jit_solution(10942274797110171761)
XLA Ops:
  0.6 29.0 %rc_block.1 = (bf16[1,128,768]{2,1,0:T(8,128)(2,1)S(1)}, bf16[1,128,1536]{2,1,0:T(8,128)(2,1)S(1)}, f32[1,1536]{1,0:T(1,128)S(1)}) custom-call(bf16[1,128,1536]{2,1,0:T(8,128)(2,1)} %feat.1, f32[1536]{0:T(1024)} %gain_in.1, bf16[5,1536,768]{2,1,0:T(8,128)(2,1)} %w.1, bf16[1,128,768]{2,1,0:T(8,128)(2,1)} %ct.1), custom_call_target="tpu_custom_call" | custom-call | tf_op jit(solution)/shard_map/rc_block/pallas_call | solution.py:312
  29.7 0.8 %hand_over.1 = (bf16[1,128,768]{2,1,0:T(8,128)(2,1)}, bf16[1,128,1536]{2,1,0:T(8,128)(2,1)}, f32[1536]{0:T(1024)}) custom-call(bf16[1,128,768]{2,1,0:T(8,128)(2,1)S(1)} %get-tuple-element.6.conv, bf16[1,128,1536]{2,1,0:T(8,128)(2,1)S(1)} %get-tuple-element.7.grad, f32[1,1536]{1,0:T(1,128)S(1)} %get-tuple-element.8.total), custom_call_target="tpu_custom_call" | custom-call | tf_op jit(solution)/shard_map/hand_over/pallas_call | solution.py:349
